TPU v7x, 512 devices: a whole 4x4x16 slice. The times are simulated.
512 devices in a mesh: pts: 16 (over z), elem: 32 (over y, x, core).
Axes of the slice: x: 4, y: 4, z: 16, core: 2. Of those that a mesh axis runs over, the one named last changes fastest.
Arguments:
- theta: float32 [1024, 1024], P('elem', 'pts'), may hold values from -3.140625 to 3.140625
- panel_rows: int32 [1024], P('elem'), may hold values from 0 to 1023, each once
- point_rows: int32 [32768], P('pts'), may hold values from 0 to 511
- point_cols: int32 [32768], P('pts'), may hold values from 0 to 255
- direct: float32 [2, 32768], P(None, 'pts'), may hold values from -3 to 3
- noise: float32 [32768], P('pts'), may hold values from 0.05 to 0.5
Outputs:
- phase_grad: float32 [1024, 1024], P('elem', 'pts')
- field: float32 [2, 32768], P(None, 'pts')
Inputs may be any that keep to these rules, and one draw needn't show every extreme that they name: `panel_rows`: each lattice row appears once.
All inputs are finite; a program needn't handle non-finite values.
Results may differ from a plain program's by a relative error of at most 0.0004.
Values sent between devices are 32-bit elements; how exact they have to be, the bound alone decides.
No kernel may reach another device: no remote copies, remote signals or barrier semaphores. Data moves between devices by JAX's collectives and lax.ppermute only.
A program may use at most 64 MiB of HBM per device.

v0:
```python
import math
import jax
import jax.numpy as jnp
from jax import lax
from jax.sharding import PartitionSpec as P

NX_EL = 1024
NY_EL = 1024
HIGH = lax.Precision.HIGHEST


def geometry(point_rows, point_cols):
    along_x = (point_rows.astype(jnp.float32) - 255.5) * 0.5
    along_y = (point_cols.astype(jnp.float32) - 127.5) * 0.5
    radius = jnp.sqrt(along_x * along_x + along_y * along_y + 1600.0)
    return (along_x / radius, along_y / radius, 80.0 / (radius * math.sqrt(NX_EL * NY_EL)))


def partial_field(slope_x, slope_y, lattice_x, lattice_y, phase_re, phase_im):
    beam_y = math.pi * slope_y[:, None] * lattice_y[None, :]
    left = jnp.concatenate([jnp.cos(beam_y), jnp.sin(beam_y)], 1)
    right = jnp.concatenate(
        [
            jnp.concatenate([phase_re.T, phase_im.T], 1),
            jnp.concatenate([-phase_im.T, phase_re.T], 1),
        ],
        0,
    )
    inner = jnp.dot(left, right, precision=HIGH, preferred_element_type=jnp.float32)
    width = phase_re.shape[0]
    inner_re = inner[:, :width]
    inner_im = inner[:, width:]
    beam_x = math.pi * slope_x[:, None] * lattice_x[None, :]
    cos_x = jnp.cos(beam_x)
    sin_x = jnp.sin(beam_x)
    return jnp.stack(
        [
            jnp.sum(cos_x * inner_re - sin_x * inner_im, 1),
            jnp.sum(cos_x * inner_im + sin_x * inner_re, 1),
        ]
    )


def surface_terms(slope_x, slope_y, q_re, q_im, lattice_x, lattice_y):
    beam_x = math.pi * slope_x[:, None] * lattice_x[None, :]
    cos_x = jnp.cos(beam_x)
    sin_x = jnp.sin(beam_x)
    weight_re = q_re[:, None] * cos_x - q_im[:, None] * sin_x
    weight_im = q_re[:, None] * sin_x + q_im[:, None] * cos_x
    beam_y = math.pi * slope_y[:, None] * lattice_y[None, :]
    left = jnp.concatenate([jnp.cos(beam_y), jnp.sin(beam_y)], 1)
    right = jnp.concatenate([weight_re, weight_im], 1)
    prod = lax.dot_general(
        left, right, (((0,), (0,)), ((), ())), precision=HIGH, preferred_element_type=jnp.float32
    )
    rows_y = lattice_y.shape[0]
    cols_x = lattice_x.shape[0]
    sum_re = prod[:rows_y, :cols_x] - prod[rows_y:, cols_x:]
    sum_im = prod[:rows_y, cols_x:] + prod[rows_y:, :cols_x]
    return jnp.concatenate([sum_re, sum_im], 1)


def block_size(points, cols_y):
    return math.gcd(points, min(points, max(256, 524288 // cols_y)))


def field_blocks(slope_x, slope_y, lattice_x, lattice_y, phase_re, phase_im):
    block = block_size(slope_x.shape[0], lattice_y.shape[0])
    count = slope_x.shape[0] // block

    def one_block(pair):
        return partial_field(pair[0], pair[1], lattice_x, lattice_y, phase_re, phase_im)

    parts = lax.map(one_block, (slope_x.reshape(count, block), slope_y.reshape(count, block)))
    return jnp.transpose(parts, (1, 0, 2)).reshape(2, count * block)


def terms_blocks(slope_x, slope_y, q_re, q_im, lattice_x, lattice_y):
    block = block_size(slope_x.shape[0], lattice_y.shape[0])
    count = slope_x.shape[0] // block
    start = jnp.zeros((lattice_y.shape[0], 2 * lattice_x.shape[0]), jnp.float32)

    def step(carry, items):
        return (
            carry + surface_terms(items[0], items[1], items[2], items[3], lattice_x, lattice_y),
            None,
        )

    items = (
        slope_x.reshape(count, block),
        slope_y.reshape(count, block),
        q_re.reshape(count, block),
        q_im.reshape(count, block),
    )
    total, unused = lax.scan(step, start, items)
    return total


def weights(field, scale, noise):
    power = noise + field[0] * field[0] + field[1] * field[1]
    return (field[0] * scale / power, -field[1] * scale / power)


def gradient(terms, phase_re, phase_im):
    cols_x = phase_re.shape[0]
    sum_re = terms[:, :cols_x].T
    sum_im = terms[:, cols_x:].T
    return -2.0 * (phase_re * sum_im + phase_im * sum_re)


def shards(theta, panel_rows, point_rows, point_cols, direct, noise):
    slope_x, slope_y, scale = geometry(point_rows, point_cols)
    phase_re = jnp.cos(theta)
    phase_im = jnp.sin(theta)
    lattice_x = panel_rows.astype(jnp.float32) - (NX_EL - 1) / 2.0
    cols_dev = theta.shape[1]
    phasors = jnp.stack([phase_re, phase_im])
    whole = lax.all_gather(phasors, "pts", axis=2, tiled=True)
    lattice_y = jnp.arange(NY_EL).astype(jnp.float32) - (NY_EL - 1) / 2.0
    partial_value = field_blocks(slope_x, slope_y, lattice_x, lattice_y, whole[0], whole[1])
    total = lax.psum(partial_value, "elem")
    field = direct + scale[None, :] * total
    q_re, q_im = weights(field, scale, noise)
    cols_here = jnp.arange(cols_dev * lax.axis_size("pts")).astype(jnp.float32) - (NY_EL - 1) / 2.0
    terms = lax.psum_scatter(
        terms_blocks(slope_x, slope_y, q_re, q_im, lattice_x, cols_here),
        "pts",
        scatter_dimension=0,
        tiled=True,
    )
    return (gradient(terms, phase_re, phase_im), field)


def solution(mesh):
    in_specs = (P("elem", "pts"), P("elem"), P("pts"), P("pts"), P(None, "pts"), P("pts"))
    out_specs = (P("elem", "pts"), P(None, "pts"))
    return jax.shard_map(shards, mesh=mesh, in_specs=in_specs, out_specs=out_specs, check_vma=False)
```

profile of v0, /device:TPU:2, one launch (start us, length us, event | category | flops | bytes accessed | tf_op | source)
XLA Modules:
  0.0 337.5 jit_solution(4195258781509086454)
XLA Ops:
  8.3 41.7 %all_gather.3 = f32[2,32,1024]{1,0,2:T(2,128)S(1)} all-gather(f32[2,32,64]{1,0,2:T(2,128)S(1)} %pad_maximum_fusion), channel_id=1, replica_groups=mesh['pts'=16,'elem'=32] {'pts'}, dimensions={2}, use_global_device_ids=true | all-gather | bytes 278528 | tf_op jit(solution)/shard_map/all_gather | solution.py:118
  49.9 0.8 fusion.38
  51.3 47.9 %while.24 = (s32[]{:T(128)}, f32[4,2,512]{2,1,0:T(2,128)S(1)}, f32[4,512]{1,0:T(4,128)S(1)}, f32[32]{0:T(128)S(1)}, f32[4,512]{1,0:T(4,128)S(1)}, /*index=5*/f32[2048,64]{1,0:T(8,128)S(1)}, s32[]{:T(128)}) while((s32[]{:T(128)}, f32[4,2,512]{2,1,0:T(2,128)S(1)}, f32[4,512]{1,0:T(4,128)S(1)}, f32[32]{0:T(128)S(1)}, ...), condition=%wide.region_3.4_spmd.clone, body=%wide.region_0.3_spmd.clone.sunk | while | flops 807029760 | bytes 9208021 | solution.py:74
  51.3 7.3 %multiply_cosine_fusion.6 = (f32[512,1024]{1,0:T(8,128)S(1)}, f32[512,1024]{1,0:T(8,128)S(1)}) fusion(f32[1024]{0:T(1024)S(1)} %convert_add_fusion.5, f32[512]{0:T(512)S(1)} %bitcast.76), kind=kLoop, calls=%fused_computation.7.clone.1 | loop fusion | flops 524288 | bytes 4200448 | tf_op jit(solution)/shard_map/while/body/eval_jaxpr/cos | solution.py:21
  58.7 4.2 %fusion.52 = f32[512,64]{0,1:T(8,128)S(1)} fusion(f32[2048,64]{1,0:T(8,128)S(1)} %get-tuple-element.375, f32[512,1024]{1,0:T(8,128)S(1)} %get-tuple-element.334, f32[512,1024]{1,0:T(8,128)S(1)} %get-tuple-element.335), kind=kOutput, calls=%fused_computation.2.clone.1 | convolution fusion | flops 806354944 | bytes 4849664 | tf_op jit(solution)/shard_map/while/body/eval_jaxpr/dot_general | solution.py:29
  63.3 7.3 %multiply_cosine_fusion.6 = (f32[512,1024]{1,0:T(8,128)S(1)}, f32[512,1024]{1,0:T(8,128)S(1)}) fusion(f32[1024]{0:T(1024)S(1)} %convert_add_fusion.5, f32[512]{0:T(512)S(1)} %bitcast.76), kind=kLoop, calls=%fused_computation.7.clone.1 | loop fusion | flops 524288 | bytes 4200448 | tf_op jit(solution)/shard_map/while/body/eval_jaxpr/cos | solution.py:21
  70.6 4.2 %fusion.52 = f32[512,64]{0,1:T(8,128)S(1)} fusion(f32[2048,64]{1,0:T(8,128)S(1)} %get-tuple-element.375, f32[512,1024]{1,0:T(8,128)S(1)} %get-tuple-element.334, f32[512,1024]{1,0:T(8,128)S(1)} %get-tuple-element.335), kind=kOutput, calls=%fused_computation.2.clone.1 | convolution fusion | flops 806354944 | bytes 4849664 | tf_op jit(solution)/shard_map/while/body/eval_jaxpr/dot_general | solution.py:29
  75.3 7.3 %multiply_cosine_fusion.6 = (f32[512,1024]{1,0:T(8,128)S(1)}, f32[512,1024]{1,0:T(8,128)S(1)}) fusion(f32[1024]{0:T(1024)S(1)} %convert_add_fusion.5, f32[512]{0:T(512)S(1)} %bitcast.76), kind=kLoop, calls=%fused_computation.7.clone.1 | loop fusion | flops 524288 | bytes 4200448 | tf_op jit(solution)/shard_map/while/body/eval_jaxpr/cos | solution.py:21
  82.6 4.2 %fusion.52 = f32[512,64]{0,1:T(8,128)S(1)} fusion(f32[2048,64]{1,0:T(8,128)S(1)} %get-tuple-element.375, f32[512,1024]{1,0:T(8,128)S(1)} %get-tuple-element.334, f32[512,1024]{1,0:T(8,128)S(1)} %get-tuple-element.335), kind=kOutput, calls=%fused_computation.2.clone.1 | convolution fusion | flops 806354944 | bytes 4849664 | tf_op jit(solution)/shard_map/while/body/eval_jaxpr/dot_general | solution.py:29
  87.2 7.3 %multiply_cosine_fusion.6 = (f32[512,1024]{1,0:T(8,128)S(1)}, f32[512,1024]{1,0:T(8,128)S(1)}) fusion(f32[1024]{0:T(1024)S(1)} %convert_add_fusion.5, f32[512]{0:T(512)S(1)} %bitcast.76), kind=kLoop, calls=%fused_computation.7.clone.1 | loop fusion | flops 524288 | bytes 4200448 | tf_op jit(solution)/shard_map/while/body/eval_jaxpr/cos | solution.py:21
  94.6 4.2 %fusion.52 = f32[512,64]{0,1:T(8,128)S(1)} fusion(f32[2048,64]{1,0:T(8,128)S(1)} %get-tuple-element.375, f32[512,1024]{1,0:T(8,128)S(1)} %get-tuple-element.334, f32[512,1024]{1,0:T(8,128)S(1)} %get-tuple-element.335), kind=kOutput, calls=%fused_computation.2.clone.1 | convolution fusion | flops 806354944 | bytes 4849664 | tf_op jit(solution)/shard_map/while/body/eval_jaxpr/dot_general | solution.py:29
  99.2 119.2 %psum.7 = f32[2,2048]{1,0:T(2,128)S(1)} all-reduce(f32[2,2048]{1,0:T(2,128)S(1)} %bitcast.82), channel_id=1, replica_groups=mesh['pts'=16,'elem'=32] {'elem'}, use_global_device_ids=true, to_apply=%region_4.5 | all-reduce | flops 4096 | bytes 32768 | tf_op jit(solution)/shard_map/psum | solution.py:121
  219.0 42.9 %while.25 = (s32[]{:T(128)}, f32[1024,64]{0,1:T(8,128)S(1)}, f32[4,512]{1,0:T(4,128)S(1)}, f32[4,512]{1,0:T(4,128)S(1)}, f32[4,512]{1,0:T(4,128)S(1)}, /*index=5...) while((s32[]{:T(128)}, f32[1024,64]{0,1:T(8,128)S(1)}, f32[4,512]{1,0:T(4,128)S(1)}, ...), condition=%wide.region_6.7_spmd.clone, body=%wide.region_5.6_spmd.clone.sunk | while | flops 807291904 | bytes 10780911 | solution.py:95
  219.3 7.3 %multiply_cosine_fusion.7 = (f32[512,1024]{1,0:T(8,128)S(1)}, f32[512,1024]{1,0:T(8,128)S(1)}) fusion(f32[1024]{0:T(1024)S(1)} %convert_add_fusion.6, f32[512]{0:T(512)S(1)} %bitcast.72), kind=kLoop, calls=%fused_computation.29.clone.1 | loop fusion | flops 524288 | bytes 4200448 | tf_op jit(solution)/shard_map/while/body/eval_jaxpr/cos | solution.py:51
  226.7 2.8 fusion.58
  230.1 7.3 %multiply_cosine_fusion.7 = (f32[512,1024]{1,0:T(8,128)S(1)}, f32[512,1024]{1,0:T(8,128)S(1)}) fusion(f32[1024]{0:T(1024)S(1)} %convert_add_fusion.6, f32[512]{0:T(512)S(1)} %bitcast.72), kind=kLoop, calls=%fused_computation.29.clone.1 | loop fusion | flops 524288 | bytes 4200448 | tf_op jit(solution)/shard_map/while/body/eval_jaxpr/cos | solution.py:51
  237.4 2.8 fusion.58
  240.8 7.3 %multiply_cosine_fusion.7 = (f32[512,1024]{1,0:T(8,128)S(1)}, f32[512,1024]{1,0:T(8,128)S(1)}) fusion(f32[1024]{0:T(1024)S(1)} %convert_add_fusion.6, f32[512]{0:T(512)S(1)} %bitcast.72), kind=kLoop, calls=%fused_computation.29.clone.1 | loop fusion | flops 524288 | bytes 4200448 | tf_op jit(solution)/shard_map/while/body/eval_jaxpr/cos | solution.py:51
  248.1 2.8 fusion.58
  251.5 7.3 %multiply_cosine_fusion.7 = (f32[512,1024]{1,0:T(8,128)S(1)}, f32[512,1024]{1,0:T(8,128)S(1)}) fusion(f32[1024]{0:T(1024)S(1)} %convert_add_fusion.6, f32[512]{0:T(512)S(1)} %bitcast.72), kind=kLoop, calls=%fused_computation.29.clone.1 | loop fusion | flops 524288 | bytes 4200448 | tf_op jit(solution)/shard_map/while/body/eval_jaxpr/cos | solution.py:51
  258.8 2.8 fusion.58
  261.8 1.0 copy.26
  262.9 66.2 %reduce-scatter.4.cloned.1.call-done = f32[64,64]{1,0:T(8,128)} async-done(((f32[1024,64]{1,0:T(8,128)}), f32[64,64]{1,0:T(8,128)}) %reduce-scatter.4.cloned.1.call-update) | async-done | bytes 16400 | tf_op jit(solution)/shard_map/reduce_scatter | solution.py:125
  329.1 0.9 fusion.34
  (71 shorter events, 6.1 us)
Async XLA Ops:
  7.2 321.9 %reduce-scatter.4.cloned.1.call-start = ((), (), s32[]{:S(2)}) async-start(), calls=%async_computation.1 | async-start | bytes 557056 | tf_op jit(solution)/shard_map/reduce_scatter | solution.py:125
  8.2 42.6 %copy-start.2 = (s32[2048]{0:T(1024)S(1)}, s32[2048]{0:T(1024)}, u32[]{:S(2)}) copy-start(s32[2048]{0:T(1024)} %param.13) | copy-start | bytes 24580
  8.3 42.6 %copy-start.3 = (s32[2048]{0:T(1024)S(1)}, s32[2048]{0:T(1024)}, u32[]{:S(2)}) copy-start(s32[2048]{0:T(1024)} %param.12) | copy-start | bytes 24580
  8.3 42.6 %copy-start.5 = (s32[32]{0:T(128)S(1)}, s32[32]{0:T(128)}, u32[]{:S(2)}) copy-start(s32[32]{0:T(128)} %param.11) | copy-start | bytes 388
  51.2 167.1 %copy-start.1 = (f32[2,2048]{1,0:T(2,128)S(1)}, f32[2,2048]{1,0:T(2,128)}, u32[]{:S(2)}) copy-start(f32[2,2048]{1,0:T(2,128)} %param.14) | copy-start | bytes 49156
  51.3 167.1 %copy-start.4 = (f32[2048]{0:T(1024)S(1)}, f32[2048]{0:T(1024)}, u32[]{:S(2)}) copy-start(f32[2048]{0:T(1024)} %param.15) | copy-start | bytes 24580
  218.4 0.6 copy-start
Sparse Core Ops, SparseCore 0:
  263.0 66.0 reduce-scatter.3
where the time goes:
time: 338 us
  blocking collectives  161 us (48%)
  waiting for transfers between devices  66.2 us (20%)
  other arithmetic  63.5 us (19%)
  matrix products  28.3 us (8%)
  between operations  14.2 us (4%)
  local copies, waits for them, and re-layouts  4.05 us (1%)
    psum x1, blocking collectives, shards(): total = lax.psum(partial_value, 'elem')  119 us
    reduce_scatter x1, waiting for transfers between devices, shards(): lax.psum_scatter(terms_blocks(slope_x, slope_y, q_re, q_im, lattice_x, co...  66.2 us
    all_gather x1, blocking collectives, shards(): whole = lax.all_gather(phasors, 'pts', axis=2, tiled=True)  41.7 us
    cos x4, other arithmetic, partial_field(): left = jnp.concatenate([jnp.cos(beam_y), jnp.sin(beam_y)], 1)  29.4 us
    cos x4, other arithmetic, surface_terms(): left = jnp.concatenate([jnp.cos(beam_y), jnp.sin(beam_y)], 1)  29.4 us
    dot_general x4, matrix products, partial_field(): jnp.dot(left, right, precision=HIGH, preferred_element_type=jnp.float32)  16.9 us
    dot_general x4, matrix products, surface_terms(): lax.dot_general(left, right, (((0,), (0,)), ((), ())), precision=HIGH, pr...  11.4 us
  transfers between devices with their start and end apart: 1, of which 1 were waited for; matrix products, arithmetic and copies ran while one was open for 0% of the time, Pallas kernels for 0%

commit v1 on v0

--- a/solution.py
+++ b/solution.py
@@ -118,7 +118,7 @@
     whole = lax.all_gather(phasors, "pts", axis=2, tiled=True)
     lattice_y = jnp.arange(NY_EL).astype(jnp.float32) - (NY_EL - 1) / 2.0
     partial_value = field_blocks(slope_x, slope_y, lattice_x, lattice_y, whole[0], whole[1])
-    total = lax.psum(partial_value, "elem")
+    total = jnp.sum(lax.all_gather(partial_value, "elem"), axis=0)
     field = direct + scale[None, :] * total
     q_re, q_im = weights(field, scale, noise)
     cols_here = jnp.arange(cols_dev * lax.axis_size("pts")).astype(jnp.float32) - (NY_EL - 1) / 2.0

time: 338 us -> 242 us (0.72)
  the two profiles are of different devices: /device:TPU:2 before, /device:TPU:4 now
where the time goes in v1:
time: 242 us
  blocking collectives  66.6 us (28%)
  waiting for transfers between devices  64.5 us (27%)
  other arithmetic  63.7 us (26%)
  matrix products  28.3 us (12%)
  between operations  14.2 us (6%)
  local copies, waits for them, and re-layouts  4.05 us (2%)
    reduce_scatter x1, waiting for transfers between devices, shards(): lax.psum_scatter(terms_blocks(slope_x, slope_y, q_re, q_im, lattice_x, co...  64.5 us
    all_gather x1, blocking collectives, shards(): whole = lax.all_gather(phasors, 'pts', axis=2, tiled=True)  41.7 us
    cos x4, other arithmetic, partial_field(): left = jnp.concatenate([jnp.cos(beam_y), jnp.sin(beam_y)], 1)  29.4 us
    cos x4, other arithmetic, surface_terms(): left = jnp.concatenate([jnp.cos(beam_y), jnp.sin(beam_y)], 1)  29.4 us
    all_gather x1, blocking collectives, shards(): total = jnp.sum(lax.all_gather(partial_value, 'elem'), axis=0)  24.9 us
    dot_general x4, matrix products, partial_field(): jnp.dot(left, right, precision=HIGH, preferred_element_type=jnp.float32)  16.9 us
    dot_general x4, matrix products, surface_terms(): lax.dot_general(left, right, (((0,), (0,)), ((), ())), precision=HIGH, pr...  11.4 us
  transfers between devices with their start and end apart: 1, of which 1 were waited for; matrix products, arithmetic and copies ran while one was open for 0% of the time, Pallas kernels for 0%

profile of v1, /device:TPU:4, one launch (start us, length us, event | category | flops | bytes accessed | tf_op | source)
XLA Modules:
  0.0 241.8 jit_solution(1602336793773625345)
XLA Ops:
  8.3 41.7 %all_gather.6 = f32[2,32,1024]{1,0,2:T(2,128)S(1)} all-gather(f32[2,32,64]{1,0,2:T(2,128)S(1)} %pad_maximum_fusion), channel_id=1, replica_groups=mesh['pts'=16,'elem'=32] {'pts'}, dimensions={2}, use_global_device_ids=true | all-gather | bytes 278528 | tf_op jit(solution)/shard_map/all_gather | solution.py:118
  49.9 0.8 fusion.38
  51.3 47.9 %while.24 = (s32[]{:T(128)}, f32[4,2,512]{2,1,0:T(2,128)S(1)}, f32[4,512]{1,0:T(4,128)S(1)}, f32[32]{0:T(128)S(1)}, f32[4,512]{1,0:T(4,128)S(1)}, /*index=5*/f32[2048,64]{1,0:T(8,128)S(1)}, s32[]{:T(128)}) while((s32[]{:T(128)}, f32[4,2,512]{2,1,0:T(2,128)S(1)}, f32[4,512]{1,0:T(4,128)S(1)}, f32[32]{0:T(128)S(1)}, ...), condition=%wide.region_3.4_spmd.clone, body=%wide.region_0.3_spmd.clone.sunk | while | flops 807029760 | bytes 9208021 | solution.py:74
  51.3 7.3 %multiply_cosine_fusion.6 = (f32[512,1024]{1,0:T(8,128)S(1)}, f32[512,1024]{1,0:T(8,128)S(1)}) fusion(f32[1024]{0:T(1024)S(1)} %convert_add_fusion.5, f32[512]{0:T(512)S(1)} %bitcast.76), kind=kLoop, calls=%fused_computation.7.clone.1 | loop fusion | flops 524288 | bytes 4200448 | tf_op jit(solution)/shard_map/while/body/eval_jaxpr/cos | solution.py:21
  58.7 4.2 %fusion.52 = f32[512,64]{0,1:T(8,128)S(1)} fusion(f32[2048,64]{1,0:T(8,128)S(1)} %get-tuple-element.375, f32[512,1024]{1,0:T(8,128)S(1)} %get-tuple-element.334, f32[512,1024]{1,0:T(8,128)S(1)} %get-tuple-element.335), kind=kOutput, calls=%fused_computation.2.clone.1 | convolution fusion | flops 806354944 | bytes 4849664 | tf_op jit(solution)/shard_map/while/body/eval_jaxpr/dot_general | solution.py:29
  63.3 7.3 %multiply_cosine_fusion.6 = (f32[512,1024]{1,0:T(8,128)S(1)}, f32[512,1024]{1,0:T(8,128)S(1)}) fusion(f32[1024]{0:T(1024)S(1)} %convert_add_fusion.5, f32[512]{0:T(512)S(1)} %bitcast.76), kind=kLoop, calls=%fused_computation.7.clone.1 | loop fusion | flops 524288 | bytes 4200448 | tf_op jit(solution)/shard_map/while/body/eval_jaxpr/cos | solution.py:21
  70.6 4.2 %fusion.52 = f32[512,64]{0,1:T(8,128)S(1)} fusion(f32[2048,64]{1,0:T(8,128)S(1)} %get-tuple-element.375, f32[512,1024]{1,0:T(8,128)S(1)} %get-tuple-element.334, f32[512,1024]{1,0:T(8,128)S(1)} %get-tuple-element.335), kind=kOutput, calls=%fused_computation.2.clone.1 | convolution fusion | flops 806354944 | bytes 4849664 | tf_op jit(solution)/shard_map/while/body/eval_jaxpr/dot_general | solution.py:29
  75.3 7.3 %multiply_cosine_fusion.6 = (f32[512,1024]{1,0:T(8,128)S(1)}, f32[512,1024]{1,0:T(8,128)S(1)}) fusion(f32[1024]{0:T(1024)S(1)} %convert_add_fusion.5, f32[512]{0:T(512)S(1)} %bitcast.76), kind=kLoop, calls=%fused_computation.7.clone.1 | loop fusion | flops 524288 | bytes 4200448 | tf_op jit(solution)/shard_map/while/body/eval_jaxpr/cos | solution.py:21
  82.6 4.2 %fusion.52 = f32[512,64]{0,1:T(8,128)S(1)} fusion(f32[2048,64]{1,0:T(8,128)S(1)} %get-tuple-element.375, f32[512,1024]{1,0:T(8,128)S(1)} %get-tuple-element.334, f32[512,1024]{1,0:T(8,128)S(1)} %get-tuple-element.335), kind=kOutput, calls=%fused_computation.2.clone.1 | convolution fusion | flops 806354944 | bytes 4849664 | tf_op jit(solution)/shard_map/while/body/eval_jaxpr/dot_general | solution.py:29
  87.2 7.3 %multiply_cosine_fusion.6 = (f32[512,1024]{1,0:T(8,128)S(1)}, f32[512,1024]{1,0:T(8,128)S(1)}) fusion(f32[1024]{0:T(1024)S(1)} %convert_add_fusion.5, f32[512]{0:T(512)S(1)} %bitcast.76), kind=kLoop, calls=%fused_computation.7.clone.1 | loop fusion | flops 524288 | bytes 4200448 | tf_op jit(solution)/shard_map/while/body/eval_jaxpr/cos | solution.py:21
  94.6 4.2 %fusion.52 = f32[512,64]{0,1:T(8,128)S(1)} fusion(f32[2048,64]{1,0:T(8,128)S(1)} %get-tuple-element.375, f32[512,1024]{1,0:T(8,128)S(1)} %get-tuple-element.334, f32[512,1024]{1,0:T(8,128)S(1)} %get-tuple-element.335), kind=kOutput, calls=%fused_computation.2.clone.1 | convolution fusion | flops 806354944 | bytes 4849664 | tf_op jit(solution)/shard_map/while/body/eval_jaxpr/dot_general | solution.py:29
  99.2 24.9 %all_gather.7 = f32[32,2,2048]{2,1,0:T(2,128)S(1)} all-gather(f32[1,2,2048]{2,1,0:T(2,128)S(1)} %bitcast.82), channel_id=1, replica_groups=mesh['pts'=16,'elem'=32] {'elem'}, dimensions={0}, use_global_device_ids=true | all-gather | bytes 540672 | tf_op jit(solution)/shard_map/all_gather | solution.py:121
  124.9 42.9 %while.25 = (s32[]{:T(128)}, f32[1024,64]{0,1:T(8,128)S(1)}, f32[4,512]{1,0:T(4,128)S(1)}, f32[4,512]{1,0:T(4,128)S(1)}, f32[4,512]{1,0:T(4,128)S(1)}, /*index=5...) while((s32[]{:T(128)}, f32[1024,64]{0,1:T(8,128)S(1)}, f32[4,512]{1,0:T(4,128)S(1)}, ...), condition=%wide.region_6.7_spmd.clone, body=%wide.region_5.6_spmd.clone.sunk | while | flops 807291904 | bytes 10780911 | solution.py:95
  125.3 7.3 %multiply_cosine_fusion.7 = (f32[512,1024]{1,0:T(8,128)S(1)}, f32[512,1024]{1,0:T(8,128)S(1)}) fusion(f32[1024]{0:T(1024)S(1)} %convert_add_fusion.6, f32[512]{0:T(512)S(1)} %bitcast.72), kind=kLoop, calls=%fused_computation.29.clone.1 | loop fusion | flops 524288 | bytes 4200448 | tf_op jit(solution)/shard_map/while/body/eval_jaxpr/cos | solution.py:51
  132.6 2.8 %fusion.58 = f32[2048,64]{0,1:T(8,128)S(1)} fusion(f32[512,1024]{1,0:T(8,128)S(1)} %get-tuple-element.347, f32[512,1024]{1,0:T(8,128)S(1)} %get-tuple-element.348, f32[512,32]{0,1:T(8,128)S(1)} %get-tuple-element.352, f32[512,32]{0,1:T(8,128)S(1)} %get-tuple-element.353), kind=kOutput, calls=%fused_computation.24.clone.1 | convolution fusion | flops 806387712 | bytes 4849664 | tf_op jit(solution)/shard_map/while/body/eval_jaxpr/dot_general | solution.py:53
  136.0 7.3 %multiply_cosine_fusion.7 = (f32[512,1024]{1,0:T(8,128)S(1)}, f32[512,1024]{1,0:T(8,128)S(1)}) fusion(f32[1024]{0:T(1024)S(1)} %convert_add_fusion.6, f32[512]{0:T(512)S(1)} %bitcast.72), kind=kLoop, calls=%fused_computation.29.clone.1 | loop fusion | flops 524288 | bytes 4200448 | tf_op jit(solution)/shard_map/while/body/eval_jaxpr/cos | solution.py:51
  143.3 2.8 %fusion.58 = f32[2048,64]{0,1:T(8,128)S(1)} fusion(f32[512,1024]{1,0:T(8,128)S(1)} %get-tuple-element.347, f32[512,1024]{1,0:T(8,128)S(1)} %get-tuple-element.348, f32[512,32]{0,1:T(8,128)S(1)} %get-tuple-element.352, f32[512,32]{0,1:T(8,128)S(1)} %get-tuple-element.353), kind=kOutput, calls=%fused_computation.24.clone.1 | convolution fusion | flops 806387712 | bytes 4849664 | tf_op jit(solution)/shard_map/while/body/eval_jaxpr/dot_general | solution.py:53
  146.7 7.3 %multiply_cosine_fusion.7 = (f32[512,1024]{1,0:T(8,128)S(1)}, f32[512,1024]{1,0:T(8,128)S(1)}) fusion(f32[1024]{0:T(1024)S(1)} %convert_add_fusion.6, f32[512]{0:T(512)S(1)} %bitcast.72), kind=kLoop, calls=%fused_computation.29.clone.1 | loop fusion | flops 524288 | bytes 4200448 | tf_op jit(solution)/shard_map/while/body/eval_jaxpr/cos | solution.py:51
  154.1 2.8 %fusion.58 = f32[2048,64]{0,1:T(8,128)S(1)} fusion(f32[512,1024]{1,0:T(8,128)S(1)} %get-tuple-element.347, f32[512,1024]{1,0:T(8,128)S(1)} %get-tuple-element.348, f32[512,32]{0,1:T(8,128)S(1)} %get-tuple-element.352, f32[512,32]{0,1:T(8,128)S(1)} %get-tuple-element.353), kind=kOutput, calls=%fused_computation.24.clone.1 | convolution fusion | flops 806387712 | bytes 4849664 | tf_op jit(solution)/shard_map/while/body/eval_jaxpr/dot_general | solution.py:53
  157.4 7.3 %multiply_cosine_fusion.7 = (f32[512,1024]{1,0:T(8,128)S(1)}, f32[512,1024]{1,0:T(8,128)S(1)}) fusion(f32[1024]{0:T(1024)S(1)} %convert_add_fusion.6, f32[512]{0:T(512)S(1)} %bitcast.72), kind=kLoop, calls=%fused_computation.29.clone.1 | loop fusion | flops 524288 | bytes 4200448 | tf_op jit(solution)/shard_map/while/body/eval_jaxpr/cos | solution.py:51
  164.8 2.8 %fusion.58 = f32[2048,64]{0,1:T(8,128)S(1)} fusion(f32[512,1024]{1,0:T(8,128)S(1)} %get-tuple-element.347, f32[512,1024]{1,0:T(8,128)S(1)} %get-tuple-element.348, f32[512,32]{0,1:T(8,128)S(1)} %get-tuple-element.352, f32[512,32]{0,1:T(8,128)S(1)} %get-tuple-element.353), kind=kOutput, calls=%fused_computation.24.clone.1 | convolution fusion | flops 806387712 | bytes 4849664 | tf_op jit(solution)/shard_map/while/body/eval_jaxpr/dot_general | solution.py:53
  167.8 1.0 copy.23
  168.8 64.5 %reduce-scatter.4.cloned.1.call-done = f32[64,64]{1,0:T(8,128)} async-done(((f32[1024,64]{1,0:T(8,128)}), f32[64,64]{1,0:T(8,128)}) %reduce-scatter.4.cloned.1.call-update) | async-done | bytes 16400 | tf_op jit(solution)/shard_map/reduce_scatter | solution.py:125
  233.3 0.9 fusion.34
  (72 shorter events, 6.3 us)
Async XLA Ops:
  7.2 226.2 %reduce-scatter.4.cloned.1.call-start = ((), (), s32[]{:S(2)}) async-start(), calls=%async_computation.1 | async-start | bytes 557056 | tf_op jit(solution)/shard_map/reduce_scatter | solution.py:125
  8.2 42.6 %copy-start.2 = (s32[2048]{0:T(1024)S(1)}, s32[2048]{0:T(1024)}, u32[]{:S(2)}) copy-start(s32[2048]{0:T(1024)} %param.13) | copy-start | bytes 24580
  8.3 42.6 %copy-start.3 = (s32[2048]{0:T(1024)S(1)}, s32[2048]{0:T(1024)}, u32[]{:S(2)}) copy-start(s32[2048]{0:T(1024)} %param.12) | copy-start | bytes 24580
  8.3 42.6 %copy-start.5 = (s32[32]{0:T(128)S(1)}, s32[32]{0:T(128)}, u32[]{:S(2)}) copy-start(s32[32]{0:T(128)} %param.11) | copy-start | bytes 388
  51.2 73.0 %copy-start.1 = (f32[2,2048]{1,0:T(2,128)S(1)}, f32[2,2048]{1,0:T(2,128)}, u32[]{:S(2)}) copy-start(f32[2,2048]{1,0:T(2,128)} %param.14) | copy-start | bytes 49156
  51.3 73.1 %copy-start.4 = (f32[2048]{0:T(1024)S(1)}, f32[2048]{0:T(1024)}, u32[]{:S(2)}) copy-start(f32[2048]{0:T(1024)} %param.15) | copy-start | bytes 24580
  124.3 0.6 copy-start
Sparse Core Ops, SparseCore 0:
  168.9 64.3 reduce-scatter.3
